TPU v7x, 128 devices: a whole 4x4x4 slice. The times are simulated.
128 devices in a mesh: seq: 16 (over y, z), batch: 8 (over x, core).
Axes of the slice: x: 4, y: 4, z: 4, core: 2. Of those that a mesh axis runs over, the one named last changes fastest.
Arguments:
- q_nope: bfloat16 [8, 64, 128, 128], P('batch', None, 'seq'), may hold values from -6 to 6
- q_rope: bfloat16 [8, 64, 128, 64], P('batch', None, 'seq'), may hold values from -8 to 8
- absorb_k: bfloat16 [128, 128, 512], P('seq'), may hold values from -0.5 to 0.5
- absorb_v: bfloat16 [128, 512, 128], P('seq'), may hold values from -0.25 to 0.25
- cache_latent: bfloat16 [8, 16384, 512], P('batch', 'seq'), may hold values from -6 to 6
- cache_rope: bfloat16 [8, 16384, 64], P('batch', 'seq'), may hold values from -8 to 8
- draft_latent: bfloat16 [8, 64, 512], P('batch'), may hold values from -6 to 6
- draft_rope: bfloat16 [8, 64, 64], P('batch'), may hold values from -6 to 6
- residual: bfloat16 [512, 7168], P('batch', 'seq'), may hold values from -1.2 to 1.2
- out_proj: bfloat16 [16384, 7168], P('seq'), may hold values from -0.046875 to 0.046875
- norm_gain: float32 [7168], replicated, may hold values from 0.5 to 1.5
- lm_head: bfloat16 [65536, 7168], P(('seq', 'batch')), may hold values from -2.4095235 to 2.4095235
- parent: int32 [8, 64], replicated, may hold values from 0 to 62, as said below
- draft_ids: int32 [8, 64], replicated, may hold values from 0 to 65535
- cache_len: int32 [8], P('batch'), may hold values from 4096 to 16384
- accept_len: int32 [8], P('batch'), may hold values from 1 to 64
Outputs:
- hidden_out: bfloat16 [512, 7168], P('batch', 'seq')
- target_logp: float32 [8, 64], P('batch')
- accepted_score: float32 [8], P('batch')
Inputs may be any that keep to these rules, and one draw needn't show every extreme that they name: parent[b, 0] = 0, and 0 <= parent[b, i] < i for i >= 1.
All inputs are finite; a program needn't handle non-finite values.
Results may differ from a plain program's by a relative error of at most 0.0095.
Values may be sent and summed in bfloat16 or wider, within the bound.
A program may use at most 256 MiB of HBM per device.

v0:
```python
import math
import jax
import jax.numpy as jnp
from jax import lax
from jax.sharding import Mesh
from jax.sharding import PartitionSpec as P

SEQ = ("seq_0", "seq_1")
BATCH = ("batch_0", "batch_1")
SEQ_BATCH = ("seq_0", "seq_1", "batch_0", "batch_1")
masked_value = -1e30
norm_epsilon = 1e-06
highest = lax.Precision.HIGHEST


def sent_together(arrays, axis, dim, along):
    ends, at = ([], 0)
    for a in arrays[:-1]:
        at += a.shape[along]
        ends.append(at)
    both = jnp.concatenate(arrays, axis=along)
    return tuple(jnp.split(lax.all_gather(both, axis, axis=dim, tiled=True), ends, axis=along))


def copy_for_each(array, axis):
    copies = jnp.broadcast_to(array, (lax.axis_size(axis), *array.shape))
    return lax.all_to_all(copies, axis, split_axis=0, concat_axis=0, tiled=True)


def over_copies(array, axis):
    everything = copy_for_each(array, axis)
    return jnp.max(everything, axis=0)


def gathered_once(array, axis):
    leaves = jax.tree.leaves(array)
    sequence = sorted(range(len(leaves)), key=lambda k: -leaves[k].size)
    width = (1, *leaves[sequence[0]].shape)[-1]
    lines = [
        jnp.pad(leaves[k].reshape(-1), (0, -leaves[k].size % width)).reshape(-1, width)
        for k in sequence
    ]
    both, at, found = (lax.all_gather(jnp.concatenate(lines), axis), 0, {})
    for k, line in zip(sequence, lines):
        piece = both[:, at : at + len(line)].reshape(len(both), -1)
        found[k] = piece[:, : leaves[k].size].reshape(-1, *leaves[k].shape)
        at += len(line)
    numbers = iter(range(len(leaves)))
    return jax.tree.map(lambda _: found[next(numbers)], array)


def combined_by_axis(array, axes, combine):
    for axis in axes:
        pieces = gathered_once(array, axis)
        array = jax.tree.map(lambda part: part[0], pieces)
        for k in range(1, lax.axis_size(axis)):
            array = combine(array, jax.tree.map(lambda part: part[k], pieces))
    return array


def ancestry_of(parents):
    draft_count = parents.shape[1]
    indices = jnp.arange(draft_count, dtype=jnp.int32)
    parent_map = (
        (parents[:, :, None] == indices[None, None, :]) & (indices[None, :, None] > 0)
    ).astype(jnp.float32)
    ancestry = jnp.broadcast_to(jnp.eye(draft_count, dtype=jnp.float32), parent_map.shape)
    for doubling in range(draft_count.bit_length() - 1):
        ancestry = ancestry + jnp.einsum("rij,rjk->rik", ancestry, parent_map, precision=highest)
        parent_map = jnp.einsum("rij,rjk->rik", parent_map, parent_map, precision=highest)
    return ancestry > 0.5


def combine_soft(earlier, later):
    top_new = jnp.maximum(earlier[0], later[0])
    mass_new = earlier[1] * jnp.exp(earlier[0] - top_new) + later[1] * jnp.exp(later[0] - top_new)
    return (top_new, mass_new, earlier[2] + later[2])


def body(
    q_nope,
    q_rope,
    absorb_k,
    absorb_v,
    cache_latent,
    cache_rope,
    draft_latent,
    draft_rope,
    residual,
    out_proj,
    norm_gain,
    lm_head,
    parent,
    draft_ids,
    cache_len,
    accept_len,
):
    requests, draft_count, local_heads, nope_width = q_nope.shape
    cache_rows = cache_latent.shape[1]
    score_scale = 1.0 / math.sqrt(nope_width + q_rope.shape[3])
    seq_index = lax.axis_index(SEQ)
    batch_index = lax.axis_index(BATCH)
    query_latent = jnp.einsum(
        "rihn,hnc->rihc", q_nope, absorb_k, preferred_element_type=jnp.float32
    ).astype(jnp.bfloat16)
    query_all, rope_all = sent_together((query_latent, q_rope), SEQ, 2, 3)
    cache_scores = jnp.einsum(
        "rihc,rtc->rhit", query_all, cache_latent, preferred_element_type=jnp.float32
    )
    cache_scores = cache_scores + jnp.einsum(
        "rihe,rte->rhit", rope_all, cache_rope, preferred_element_type=jnp.float32
    )
    positions = seq_index * cache_rows + jnp.arange(cache_rows, dtype=jnp.int32)
    in_cache = positions[None, :] < cache_len[:, None]
    cache_scores = jnp.where(in_cache[:, None, None, :], cache_scores * score_scale, masked_value)
    tree_scores = jnp.einsum(
        "rihc,rjc->rhij", query_all, draft_latent, preferred_element_type=jnp.float32
    )
    tree_scores = tree_scores + jnp.einsum(
        "rihe,rje->rhij", rope_all, draft_rope, preferred_element_type=jnp.float32
    )
    own_parents = lax.dynamic_slice_in_dim(parent, batch_index * requests, requests, 0)
    ancestry = ancestry_of(own_parents)
    tree_scores = jnp.where(ancestry[:, None, :, :], tree_scores * score_scale, masked_value)
    local_top = jnp.maximum(jnp.max(cache_scores, axis=3), jnp.max(tree_scores, axis=3))
    row_top = over_copies(local_top, SEQ)
    cache_weights = jnp.exp(cache_scores - row_top[..., None])
    weight_sum = jnp.sum(cache_weights, axis=3)
    partial_value = jnp.einsum(
        "rhit,rtc->rhic",
        cache_weights.astype(jnp.bfloat16),
        cache_latent,
        preferred_element_type=jnp.float32,
    )
    head_first = seq_index * local_heads
    tree_mine = lax.dynamic_slice_in_dim(tree_scores, head_first, local_heads, 1)
    top_mine = lax.dynamic_slice_in_dim(row_top, head_first, local_heads, 1)
    tree_weights = jnp.exp(tree_mine - top_mine[..., None])
    tree_out = jnp.einsum(
        "rhij,rjc->rhic",
        tree_weights.astype(jnp.bfloat16),
        draft_latent,
        preferred_element_type=jnp.float32,
    )
    latent_sum, weight_total = (
        lax.psum_scatter(partial_value, SEQ, scatter_dimension=1, tiled=True),
        lax.psum_scatter(weight_sum, SEQ, scatter_dimension=1, tiled=True),
    )
    summed = jnp.einsum(
        "rhic,hcn->rhin", latent_sum + tree_out, absorb_v, preferred_element_type=jnp.float32
    )
    weight_total = weight_total + jnp.sum(tree_weights, axis=3)
    head_out = (summed / weight_total[..., None]).astype(jnp.bfloat16)
    head_rows = jnp.transpose(head_out, (0, 2, 1, 3)).reshape(
        requests * draft_count, local_heads * head_out.shape[3]
    )
    branch_term = jnp.dot(head_rows, out_proj, preferred_element_type=jnp.float32)
    width_local = residual.shape[1]
    feature_first = seq_index * width_local
    residual_wide = lax.dynamic_update_slice_in_dim(
        jnp.zeros_like(branch_term), residual.astype(jnp.float32), feature_first, 1
    )
    stream = lax.psum(branch_term + residual_wide, SEQ)
    square = jnp.sum(stream * stream, axis=1)
    normed = (
        stream * lax.rsqrt(square / stream.shape[1] + norm_epsilon)[:, None] * norm_gain
    ).astype(jnp.bfloat16)
    hidden_out = lax.dynamic_slice_in_dim(stream, feature_first, width_local, 1).astype(
        jnp.bfloat16
    )
    vocab_rows = lm_head.shape[0]
    vocab_first = lax.axis_index(SEQ_BATCH) * vocab_rows
    logits = jnp.einsum(
        "rd,vd->rv",
        lax.all_gather(normed, BATCH, axis=0, tiled=True),
        lm_head,
        preferred_element_type=jnp.float32,
    )
    request_total = parent.shape[0]
    parent_rows = (
        jnp.arange(request_total, dtype=jnp.int32)[:, None] * draft_count + parent
    ).reshape(-1)
    source = logits[parent_rows]
    column = jnp.arange(vocab_rows, dtype=jnp.int32) + vocab_first
    picked = jnp.sum(
        jnp.where(column[None, :] == draft_ids.reshape(-1)[:, None], source, 0.0), axis=1
    )
    local_best = jnp.max(logits, axis=1)
    local_mass = jnp.sum(jnp.exp(logits - local_best[:, None]), axis=1)
    best, exp_mass, chosen = combined_by_axis(
        (local_best, local_mass, picked), SEQ_BATCH, combine_soft
    )
    log_total = best + jnp.log(exp_mass)
    target_all = (chosen - log_total[parent_rows]).reshape(request_total, draft_count)
    target_logp = lax.dynamic_slice_in_dim(target_all, batch_index * requests, requests, 0)
    accepted_score = jnp.sum(
        jnp.where(
            jnp.arange(draft_count, dtype=jnp.int32)[None, :] < accept_len[:, None],
            target_logp,
            0.0,
        ),
        axis=1,
    )
    return (hidden_out, target_logp, accepted_score)


def solution(mesh):
    split = Mesh(mesh.devices.reshape(4, 4, 4, 2), ("seq_0", "seq_1", "batch_0", "batch_1"))
    in_specs = (
        P(BATCH, None, SEQ, None),
        P(BATCH, None, SEQ, None),
        P(SEQ, None, None),
        P(SEQ, None, None),
        P(BATCH, SEQ, None),
        P(BATCH, SEQ, None),
        P(BATCH, None, None),
        P(BATCH, None, None),
        P(BATCH, SEQ),
        P(SEQ, None),
        P(),
        P(SEQ_BATCH, None),
        P(),
        P(),
        P(BATCH),
        P(BATCH),
    )
    out_specs = (P(BATCH, SEQ), P(BATCH, None), P(BATCH))
    return jax.shard_map(body, mesh=split, in_specs=in_specs, out_specs=out_specs, check_vma=False)
```

profile of v0, /device:TPU:1, one launch (start us, length us, event | category | flops | bytes accessed | tf_op | source)
XLA Modules:
  0.0 529.6 jit_solution(17929896783594325636)
XLA Ops:
  7.2 1.0 copy.41
  8.2 1.6 fusion.16
  9.9 0.9 maximum_bitcast_fusion
  11.5 0.7 fusion.88
  12.2 0.2 fusion.39
  12.5 0.2 convolution_add_fusion.5
  12.7 0.2 fusion.99
  12.8 0.2 convolution_add_fusion.4
  13.2 0.2 convolution_add_fusion.3
  13.9 0.2 convolution_add_fusion.1
  14.0 0.2 fusion.17
  14.3 80.4 %all-gather.11.cloned.1.call-done = bf16[1,64,128,576]{3,1,0,2:T(8,128)(2,1)} async-done(((bf16[1,64,8,576]{3,1,0,2:T(8,128)(2,1)}), bf16[1,64,128,576]{3,1,0,2:T(8,128)(2,1)}) %all-gather.11.cloned.1.call-update) | async-done | bytes 9437200 | tf_op jit(solution)/shard_map/all_gather | solution.py:22
  94.7 1.8 split.9
  96.5 2.9 copy.69
  99.4 7.5 %fusion.10 = f32[64,128,64]{0,2,1:T(8,128)S(1)} fusion(bf16[1,64,512]{2,1,0:T(8,128)(2,1)S(1)} %copy-done.5, bf16[1,64,128,576]{3,1,0,2:T(8,128)(2,1)} %all-gather.11.cloned.1.call-done), kind=kOutput, calls=%fused_computation.11 | convolution fusion | flops 536870912 | bytes 10551296 | tf_op jit(solution)/shard_map/rihc,rjc->rhij/dot_general | solution.py:116
  106.9 5.8 %fusion.97 = (f32[128,64]{1,0:T(8,128)S(1)}, f32[1,128,64,64]{2,3,1,0:T(8,128)}) fusion(f32[64,128,64]{0,2,1:T(8,128)S(1)} %fusion.10, bf16[1,64,64]{2,1,0:T(8,128)(2,1)S(1)} %copy-done.8, bf16[1,64,128,576]{3,1,0,2:T(8,128)(2,1)} %all-gather.11.cloned.1.call-done, pred[64,64]{0,1:T(8,128)(4,1)S(1)} %copy.45), kind=kOutput, calls=%fused_computation.169 | convolution fusion | flops 69197824 | bytes 6336512 | tf_op jit(solution)/shard_map/rihe,rje->rhij/dot_general | solution.py:119
  112.8 7.7 %split.8 = bf16[1,64,128,512]{3,1,0,2:T(8,128)(2,1)} slice(bf16[1,64,128,576]{3,1,0,2:T(8,128)(2,1)} %all-gather.11.cloned.1.call-done), slice={[0:1], [0:64], [0:128], [0:512]} | slice | bytes 16777216 | tf_op jit(solution)/shard_map/split | solution.py:22
  120.5 30.0 %fusion.12 = f32[64,128,1024]{2,1,0:T(8,128)} fusion(bf16[1,64,128,512]{3,1,0,2:T(8,128)(2,1)} %split.8, bf16[1,1024,512]{2,1,0:T(8,128)(2,1)S(1)} %copy-done), kind=kOutput, calls=%fused_computation.14 | convolution fusion | flops 8589934592 | bytes 42991616 | tf_op jit(solution)/shard_map/rihc,rtc->rhit/dot_general | solution.py:107
  150.5 21.9 %fusion.96 = (f32[128,64]{0,1:T(8,128)S(1)}, f32[1,128,64,1024]{3,1,2,0:T(8,128)}) fusion(f32[64,128,1024]{2,1,0:T(8,128)} %fusion.12, bf16[1,1024,64]{1,2,0:T(8,128)(2,1)S(1)} %copy-done.4, bf16[1,64,128,64]{2,3,1,0:T(8,128)(2,1)S(1)} %copy-done.3, pred[1024]{0:T(1024)(128)(4,1)S(1)} %add_compare_fusion), kind=kOutput, calls=%fused_computation.168 | convolution fusion | flops 1107288064 | bytes 68322304 | tf_op jit(solution)/shard_map/rihe,rte->rhit/dot_general | solution.py:110
  172.5 15.1 %all_to_all.5 = f32[16,1,128,64]{2,3,1,0:T(8,128)S(1)} all-to-all(f32[16,1,128,64]{2,3,1,0:T(8,128)S(1)} %broadcast_in_dim.37), channel_id=1, replica_groups=mesh['seq_0'=4,'seq_1'=4,'batch_0'=4,'batch_1'=2] {'seq_0','seq_1'}, dimensions={0} | all-to-all | bytes 1048576 | tf_op jit(solution)/shard_map/all_to_all | solution.py:27
  187.7 18.7 %fusion.7 = f32[1,128,64,512]{3,1,2,0:T(8,128)} fusion(f32[1,128,64,1024]{3,1,2,0:T(8,128)} %get-tuple-element.19, f32[128,64]{0,1:T(8,128)S(1)} %reduce_max.38, bf16[1,1024,512]{2,1,0:T(8,128)(2,1)S(1)} %copy-done), kind=kOutput, calls=%fused_computation.10 | convolution fusion | flops 8606711808 | bytes 51412992 | tf_op jit(solution)/shard_map/rhit,rtc->rhic/dot_general | solution.py:129
  206.5 0.6 copy-done.12
  207.0 0.6 dynamic-slice.5
  208.4 1.0 fusion.24
  209.5 14.9 %fusion.1 = f32[128,64]{0,1:T(8,128)S(1)} fusion(f32[1,128,64,1024]{3,1,2,0:T(8,128)} %get-tuple-element.19, f32[128,64]{0,1:T(8,128)S(1)} %reduce_max.38), kind=kLoop, calls=%fused_computation.5 | loop fusion | flops 16769024 | bytes 33619968 | tf_op jit(solution)/shard_map/reduce_sum | solution.py:128
  224.6 58.5 %all-reduce = f32[1,128,64]{2,1,0:T(8,128)S(1)} all-reduce(f32[1,128,64]{2,1,0:T(8,128)S(1)} %copy.53), channel_id=7, replica_groups=mesh['seq_0'=4,'seq_1'=4,'batch_0'=4,'batch_1'=2] {'seq_0','seq_1'}, use_global_device_ids=true, to_apply=%region_5.6.clone | all-reduce | flops 8192 | bytes 65536
  283.4 33.9 %reduce-scatter.3.cloned.1.call-done = f32[1,8,64,512]{3,1,2,0:T(8,128)} async-done(((f32[1,128,64,512]{3,1,2,0:T(8,128)}), f32[1,8,64,512]{3,1,2,0:T(8,128)}) %reduce-scatter.3.cloned.1.call-update) | async-done | bytes 1048592 | tf_op jit(solution)/shard_map/reduce_scatter | solution.py:146
  317.3 1.5 fusion.15
  318.9 0.4 fusion.19
  319.4 7.9 %fusion.27 = f32[64,7168]{1,0:T(8,128)S(1)} fusion(bf16[1024,7168]{1,0:T(8,128)(2,1)} %param.25, bf16[8,8,8,128]{3,2,1,0:T(8,128)(2,1)S(1)} %bitcast.377), kind=kOutput, calls=%fused_computation.45 | convolution fusion | flops 939524096 | bytes 16646144 | tf_op jit(solution)/shard_map/dot_general | solution.py:157
  327.4 1.1 add.352
  328.5 1.2 copy-done.2
  329.8 88.2 %all-reduce.3.cloned.1.call-done = f32[64,7168]{1,0:T(8,128)} async-done(((f32[64,7168]{1,0:T(8,128)}), f32[64,7168]{1,0:T(8,128)}) %all-reduce.3.cloned.1.call-update) | async-done | bytes 1835024 | tf_op jit(solution)/shard_map/psum | solution.py:163
  418.0 1.7 multiply_reduce_fusion
  419.7 2.7 multiply_convert_fusion
  423.3 1.6 dynamic-slice_convert_fusion
  425.0 43.8 %all-gather.13.cloned.1.call-done = bf16[512,7168]{1,0:T(8,128)(2,1)} async-done(((bf16[64,7168]{1,0:T(8,128)(2,1)}), bf16[512,7168]{1,0:T(8,128)(2,1)}) %all-gather.13.cloned.1.call-update) | async-done | bytes 7340048 | tf_op jit(solution)/shard_map/all_gather | solution.py:175
  468.8 8.5 %fusion.98 = (f32[512]{0:T(512)S(1)}, f32[512,512]{0,1:T(8,128)S(1)}) fusion(bf16[512,7168]{1,0:T(8,128)(2,1)} %all-gather.13.cloned.1.call-done, bf16[512,7168]{1,0:T(8,128)(2,1)} %param.27), kind=kOutput, calls=%fused_computation.170 | convolution fusion | flops 3758358016 | bytes 15730688 | tf_op jit(solution)/shard_map/rd,vd->rv/dot_general | solution.py:173
  477.3 0.3 copy.58
  477.6 0.2 exponential_reduce_fusion
  477.8 1.6 gather_fusion
  479.5 0.3 select_reduce_fusion
  479.7 9.6 %all-gather.4 = f32[4,3,512]{2,1,0:T(4,128)S(1)} all-gather(f32[1,3,512]{2,1,0:T(4,128)S(1)} %maximum_bitcast_fusion.1), channel_id=2, replica_groups=mesh['seq_0'=4,'seq_1'=4,'batch_0'=4,'batch_1'=2] {'seq_0'}, dimensions={0}, use_global_device_ids=true | all-gather | bytes 30720 | tf_op jit(solution)/shard_map/all_gather | solution.py:43
  489.4 9.5 %all-gather.5 = f32[4,3,512]{2,1,0:T(4,128)S(1)} all-gather(f32[1,3,512]{2,1,0:T(4,128)S(1)} %maximum_bitcast_fusion.2), channel_id=3, replica_groups=mesh['seq_0'=4,'seq_1'=4,'batch_0'=4,'batch_1'=2] {'seq_1'}, dimensions={0}, use_global_device_ids=true | all-gather | bytes 30720 | tf_op jit(solution)/shard_map/all_gather | solution.py:43
  498.9 9.0 %all-gather.6 = f32[4,3,512]{2,1,0:T(4,128)S(1)} all-gather(f32[1,3,512]{2,1,0:T(4,128)S(1)} %maximum_bitcast_fusion.3), channel_id=4, replica_groups=mesh['seq_0'=4,'seq_1'=4,'batch_0'=4,'batch_1'=2] {'batch_0'}, dimensions={0}, use_global_device_ids=true | all-gather | bytes 30720 | tf_op jit(solution)/shard_map/all_gather | solution.py:43
  508.0 10.2 %all-gather.7 = f32[2,3,512]{2,1,0:T(4,128)S(1)} all-gather(f32[1,3,512]{2,1,0:T(4,128)S(1)} %maximum_bitcast_fusion.4), channel_id=5, replica_groups=mesh['seq_0'=4,'seq_1'=4,'batch_0'=4,'batch_1'=2] {'batch_1'}, dimensions={0}, use_global_device_ids=true | all-gather | bytes 18432 | tf_op jit(solution)/shard_map/all_gather | solution.py:43
  518.3 3.5 gather_fusion.1
  521.9 1.1 fusion.89
  (77 shorter events, 2.6 us)
Async XLA Ops:
  7.2 113.3 %copy-start = (bf16[1,1024,512]{2,1,0:T(8,128)(2,1)S(1)}, bf16[1,1024,512]{2,1,0:T(8,128)(2,1)}, u32[]{:S(2)}) copy-start(bf16[1,1024,512]{2,1,0:T(8,128)(2,1)} %param.20) | copy-start | bytes 3145732
  7.2 92.3 %copy-start.5 = (bf16[1,64,512]{2,1,0:T(8,128)(2,1)S(1)}, bf16[1,64,512]{2,1,0:T(8,128)(2,1)}, u32[]{:S(2)}) copy-start(bf16[1,64,512]{2,1,0:T(8,128)(2,1)} %param.22) | copy-start | bytes 196612
  7.2 87.5 %all-gather.11.cloned.1.call-start = ((), (), s32[]{:S(2)}) async-start(), calls=%async_computation.2 | async-start | bytes 11141120 | tf_op jit(solution)/shard_map/all_gather | solution.py:22
  10.8 306.5 %reduce-scatter.3.cloned.1.call-start = ((), (), s32[]{:S(2)}) async-start(), calls=%async_computation.3 | async-start | bytes 17825792 | tf_op jit(solution)/shard_map/reduce_scatter | solution.py:146
  96.5 10.4 %copy-start.8 = (bf16[1,64,64]{2,1,0:T(8,128)(2,1)S(1)}, bf16[1,64,64]{2,1,0:T(8,128)(2,1)}, u32[]{:S(2)}) copy-start(bf16[1,64,64]{2,1,0:T(8,128)(2,1)} %param.23) | copy-start | bytes 24580
  120.5 30.0 %copy-start.3 = (bf16[1,64,128,64]{2,3,1,0:T(8,128)(2,1)S(1)}, bf16[1,64,128,64]{2,3,1,0:T(8,128)(2,1)}, u32[]{:S(2)}) copy-start(bf16[1,64,128,64]{2,3,1,0:T(8,128)(2,1)} %copy.69) | copy-start | bytes 3145732
  120.5 30.0 %copy-start.4 = (bf16[1,1024,64]{1,2,0:T(8,128)(2,1)S(1)}, bf16[1,1024,64]{1,2,0:T(8,128)(2,1)}, u32[]{:S(2)}) copy-start(bf16[1,1024,64]{1,2,0:T(8,128)(2,1)} %param.21) | copy-start | bytes 393220
  206.4 0.7 copy-start.12
  206.4 211.5 %all-reduce.3.cloned.1.call-start = ((), (), s32[]{:S(2)}) async-start(), calls=%async_computation.4 | async-start | bytes 3670016 | tf_op jit(solution)/shard_map/psum | solution.py:163
  209.5 109.3 %copy-start.11 = (bf16[8,512,128]{2,1,0:T(8,128)(2,1)S(1)}, bf16[8,512,128]{2,1,0:T(8,128)(2,1)}, u32[]{:S(2)}) copy-start(bf16[8,512,128]{2,1,0:T(8,128)(2,1)} %param.19) | copy-start | bytes 3145732
  319.3 7.9 %copy-start.6 = (bf16[64,448]{1,0:T(8,128)(2,1)S(1)}, bf16[64,448]{1,0:T(8,128)(2,1)}, u32[]{:S(2)}) copy-start(bf16[64,448]{1,0:T(8,128)(2,1)} %param.24) | copy-start | bytes 172036
  319.3 100.3 %copy-start.7 = (f32[7168]{0:T(1024)S(1)}, f32[7168]{0:T(1024)}, u32[]{:S(2)}) copy-start(f32[7168]{0:T(1024)} %param.26) | copy-start | bytes 86020
  319.4 103.7 %copy-start.9 = (s32[8,64]{1,0:T(8,128)S(1)}, s32[8,64]{1,0:T(8,128)}, u32[]{:S(2)}) copy-start(s32[8,64]{1,0:T(8,128)} %param.29) | copy-start | bytes 6148
  319.4 103.8 %copy-start.10 = (s32[8,64]{1,0:T(8,128)S(1)}, s32[8,64]{1,0:T(8,128)}, u32[]{:S(2)}) copy-start(s32[8,64]{1,0:T(8,128)} %param.28) | copy-start | bytes 6148
  328.5 1.3 copy-start.2
  329.7 139.0 %all-gather.13.cloned.1.call-start = ((), (), s32[]{:S(2)}) async-start(), calls=%async_computation.5 | async-start | bytes 8257536 | tf_op jit(solution)/shard_map/all_gather | solution.py:175
  468.8 54.3 %copy-start.1 = (bf16[1,1024,512]{2,1,0:T(8,128)(2,1)S(1)}, bf16[1,1024,512]{2,1,0:T(8,128)(2,1)}, u32[]{:S(2)}) copy-start(bf16[1,1024,512]{2,1,0:T(8,128)(2,1)} %param.20) | copy-start | bytes 3145732
Sparse Core Ops, SparseCore 0:
  10.9 83.7 all-gather.10
  206.5 110.7 reduce-scatter.2
  329.9 88.0 all-reduce.2
  422.5 46.2 all-gather.12
where the time goes:
time: 530 us
  waiting for transfers between devices  246 us (46%)
  blocking collectives  112 us (21%)
  matrix products  106 us (20%)
  local copies, waits for them, and re-layouts  26 us (5%)
  other arithmetic  23.3 us (4%)
  between operations  16.1 us (3%)
    psum x1, waiting for transfers between devices, body(): stream = lax.psum(branch_term + residual_wide, SEQ)  88.2 us
    all_gather x1, waiting for transfers between devices, sent_together(): lax.all_gather(both, axis, axis=dim, tiled=True)  80.4 us
    unnamed x1, blocking collectives  58.5 us
    all_gather x1, waiting for transfers between devices, body(): lax.all_gather(normed, BATCH, axis=0, tiled=True)  43.8 us
    all_gather x4, blocking collectives, gathered_once(): both, at, found = (lax.all_gather(jnp.concatenate(lines), axis), 0, {})  38.3 us
    reduce_scatter x1, waiting for transfers between devices, body(): lax.psum_scatter(partial_value, SEQ, scatter_dimension=1, tiled=True)  33.9 us
    dot_general x1, matrix products, body(): jnp.einsum('rihc,rtc->rhit', query_all, cache_latent, preferred_element_t...  30 us
    dot_general x1, matrix products, body(): jnp.einsum('rihe,rte->rhit', rope_all, cache_rope, preferred_element_type...  21.9 us
  transfers between devices with their start and end apart: 4, of which 4 were waited for; matrix products, arithmetic and copies ran while one was open for 4% of the time, Pallas kernels for 0%

commit v1 on v0

--- a/solution.py
+++ b/solution.py
@@ -160,7 +160,8 @@
     residual_wide = lax.dynamic_update_slice_in_dim(
         jnp.zeros_like(branch_term), residual.astype(jnp.float32), feature_first, 1
     )
-    stream = lax.psum(branch_term + residual_wide, SEQ)
+    local_block = branch_term + residual_wide
+    stream = lax.psum(lax.psum(local_block, "seq_0"), "seq_1")
     square = jnp.sum(stream * stream, axis=1)
     normed = (
         stream * lax.rsqrt(square / stream.shape[1] + norm_epsilon)[:, None] * norm_gain

time: 530 us -> 552 us (1.042)
  waiting for transfers between devices: 246 us -> 268 us
    psum x1 -> x2, waiting for transfers between devices: 88.2 us -> 111 us  [body(): stream = lax.psum(lax.psum(local_block, 'seq_0'), 'seq_1')]
  transfers between devices with their start and end apart: 4 -> 5, of which waited for: 4 -> 5; matrix products, arithmetic and copies ran while one was open for 4% -> 4% of each run, Pallas kernels for 0% -> 0%
where the time goes in v1:
time: 552 us
  waiting for transfers between devices  268 us (49%)
  blocking collectives  112 us (20%)
  matrix products  106 us (19%)
  local copies, waits for them, and re-layouts  25.9 us (5%)
  other arithmetic  23.3 us (4%)
  between operations  16.2 us (3%)
    psum x2, waiting for transfers between devices, body(): stream = lax.psum(lax.psum(local_block, 'seq_0'), 'seq_1')  111 us
    all_gather x1, waiting for transfers between devices, sent_together(): lax.all_gather(both, axis, axis=dim, tiled=True)  80.4 us
    unnamed x1, blocking collectives  58.5 us
    all_gather x1, waiting for transfers between devices, body(): lax.all_gather(normed, BATCH, axis=0, tiled=True)  43 us
    all_gather x4, blocking collectives, gathered_once(): both, at, found = (lax.all_gather(jnp.concatenate(lines), axis), 0, {})  38.3 us
    reduce_scatter x1, waiting for transfers between devices, body(): lax.psum_scatter(partial_value, SEQ, scatter_dimension=1, tiled=True)  33.9 us
    dot_general x1, matrix products, body(): jnp.einsum('rihc,rtc->rhit', query_all, cache_latent, preferred_element_t...  30 us
    dot_general x1, matrix products, body(): jnp.einsum('rihe,rte->rhit', rope_all, cache_rope, preferred_element_type...  21.9 us
  transfers between devices with their start and end apart: 5, of which 5 were waited for; matrix products, arithmetic and copies ran while one was open for 4% of the time, Pallas kernels for 0%

profile of v1, /device:TPU:1, one launch (start us, length us, event | category | flops | bytes accessed | tf_op | source)
XLA Modules:
  0.0 551.6 jit_solution(4770908249126107364)
XLA Ops:
  7.2 1.0 copy.41
  8.2 1.6 fusion.16
  9.9 0.9 maximum_bitcast_fusion
  11.5 0.7 fusion.88
  12.2 0.2 fusion.39
  12.5 0.2 convolution_add_fusion.5
  12.7 0.2 fusion.99
  12.8 0.2 convolution_add_fusion.4
  13.9 0.2 convolution_add_fusion.1
  14.0 0.2 fusion.17
  14.3 80.4 %all-gather.11.cloned.1.call-done = bf16[1,64,128,576]{3,1,0,2:T(8,128)(2,1)} async-done(((bf16[1,64,8,576]{3,1,0,2:T(8,128)(2,1)}), bf16[1,64,128,576]{3,1,0,2:T(8,128)(2,1)}) %all-gather.11.cloned.1.call-update) | async-done | bytes 9437200 | tf_op jit(solution)/shard_map/all_gather | solution.py:22
  94.7 1.8 split.9
  96.5 2.9 copy.69
  99.4 7.5 %fusion.10 = f32[64,128,64]{0,2,1:T(8,128)S(1)} fusion(bf16[1,64,512]{2,1,0:T(8,128)(2,1)S(1)} %copy-done.5, bf16[1,64,128,576]{3,1,0,2:T(8,128)(2,1)} %all-gather.11.cloned.1.call-done), kind=kOutput, calls=%fused_computation.11 | convolution fusion | flops 536870912 | bytes 10551296 | tf_op jit(solution)/shard_map/rihc,rjc->rhij/dot_general | solution.py:116
  106.9 5.8 %fusion.97 = (f32[128,64]{1,0:T(8,128)S(1)}, f32[1,128,64,64]{2,3,1,0:T(8,128)}) fusion(f32[64,128,64]{0,2,1:T(8,128)S(1)} %fusion.10, bf16[1,64,64]{2,1,0:T(8,128)(2,1)S(1)} %copy-done.8, bf16[1,64,128,576]{3,1,0,2:T(8,128)(2,1)} %all-gather.11.cloned.1.call-done, pred[64,64]{0,1:T(8,128)(4,1)S(1)} %copy.45), kind=kOutput, calls=%fused_computation.169 | convolution fusion | flops 69197824 | bytes 6336512 | tf_op jit(solution)/shard_map/rihe,rje->rhij/dot_general | solution.py:119
  112.8 7.7 %split.8 = bf16[1,64,128,512]{3,1,0,2:T(8,128)(2,1)} slice(bf16[1,64,128,576]{3,1,0,2:T(8,128)(2,1)} %all-gather.11.cloned.1.call-done), slice={[0:1], [0:64], [0:128], [0:512]} | slice | bytes 16777216 | tf_op jit(solution)/shard_map/split | solution.py:22
  120.5 30.0 %fusion.12 = f32[64,128,1024]{2,1,0:T(8,128)} fusion(bf16[1,64,128,512]{3,1,0,2:T(8,128)(2,1)} %split.8, bf16[1,1024,512]{2,1,0:T(8,128)(2,1)S(1)} %copy-done), kind=kOutput, calls=%fused_computation.14 | convolution fusion | flops 8589934592 | bytes 42991616 | tf_op jit(solution)/shard_map/rihc,rtc->rhit/dot_general | solution.py:107
  150.5 21.9 %fusion.96 = (f32[128,64]{0,1:T(8,128)S(1)}, f32[1,128,64,1024]{3,1,2,0:T(8,128)}) fusion(f32[64,128,1024]{2,1,0:T(8,128)} %fusion.12, bf16[1,1024,64]{1,2,0:T(8,128)(2,1)S(1)} %copy-done.4, bf16[1,64,128,64]{2,3,1,0:T(8,128)(2,1)S(1)} %copy-done.3, pred[1024]{0:T(1024)(128)(4,1)S(1)} %add_compare_fusion), kind=kOutput, calls=%fused_computation.168 | convolution fusion | flops 1107288064 | bytes 68322304 | tf_op jit(solution)/shard_map/rihe,rte->rhit/dot_general | solution.py:110
  172.5 15.1 %all_to_all.5 = f32[16,1,128,64]{2,3,1,0:T(8,128)S(1)} all-to-all(f32[16,1,128,64]{2,3,1,0:T(8,128)S(1)} %broadcast_in_dim.37), channel_id=1, replica_groups=mesh['seq_0'=4,'seq_1'=4,'batch_0'=4,'batch_1'=2] {'seq_0','seq_1'}, dimensions={0} | all-to-all | bytes 1048576 | tf_op jit(solution)/shard_map/all_to_all | solution.py:27
  187.7 18.7 %fusion.7 = f32[1,128,64,512]{3,1,2,0:T(8,128)} fusion(f32[1,128,64,1024]{3,1,2,0:T(8,128)} %get-tuple-element.19, f32[128,64]{0,1:T(8,128)S(1)} %reduce_max.38, bf16[1,1024,512]{2,1,0:T(8,128)(2,1)S(1)} %copy-done), kind=kOutput, calls=%fused_computation.10 | convolution fusion | flops 8606711808 | bytes 51412992 | tf_op jit(solution)/shard_map/rhit,rtc->rhic/dot_general | solution.py:129
  206.5 0.6 copy-done.12
  207.0 0.6 dynamic-slice.5
  208.4 1.0 fusion.24
  209.5 14.9 %fusion.1 = f32[128,64]{0,1:T(8,128)S(1)} fusion(f32[1,128,64,1024]{3,1,2,0:T(8,128)} %get-tuple-element.19, f32[128,64]{0,1:T(8,128)S(1)} %reduce_max.38), kind=kLoop, calls=%fused_computation.5 | loop fusion | flops 16769024 | bytes 33619968 | tf_op jit(solution)/shard_map/reduce_sum | solution.py:128
  224.6 58.5 %all-reduce = f32[1,128,64]{2,1,0:T(8,128)S(1)} all-reduce(f32[1,128,64]{2,1,0:T(8,128)S(1)} %copy.53), channel_id=7, replica_groups=mesh['seq_0'=4,'seq_1'=4,'batch_0'=4,'batch_1'=2] {'seq_0','seq_1'}, use_global_device_ids=true, to_apply=%region_5.6.clone | all-reduce | flops 8192 | bytes 65536
  283.4 33.9 %reduce-scatter.3.cloned.1.call-done = f32[1,8,64,512]{3,1,2,0:T(8,128)} async-done(((f32[1,128,64,512]{3,1,2,0:T(8,128)}), f32[1,8,64,512]{3,1,2,0:T(8,128)}) %reduce-scatter.3.cloned.1.call-update) | async-done | bytes 1048592 | tf_op jit(solution)/shard_map/reduce_scatter | solution.py:146
  317.3 1.5 fusion.15
  318.9 0.4 fusion.19
  319.4 7.9 %fusion.27 = f32[64,7168]{1,0:T(8,128)S(1)} fusion(bf16[1024,7168]{1,0:T(8,128)(2,1)} %param.25, bf16[8,8,8,128]{3,2,1,0:T(8,128)(2,1)S(1)} %bitcast.377), kind=kOutput, calls=%fused_computation.45 | convolution fusion | flops 939524096 | bytes 16646144 | tf_op jit(solution)/shard_map/dot_general | solution.py:157
  327.4 1.1 add.354
  328.5 1.2 copy-done.2
  329.8 54.3 %all-reduce.4.cloned.1.call-done = f32[64,7168]{1,0:T(8,128)} async-done(((f32[64,7168]{1,0:T(8,128)}), f32[64,7168]{1,0:T(8,128)}) %all-reduce.4.cloned.1.call-update) | async-done | bytes 1835024 | tf_op jit(solution)/shard_map/psum | solution.py:164
  384.2 56.7 %all-reduce.6.cloned.1.call-done = f32[64,7168]{1,0:T(8,128)} async-done(((f32[64,7168]{1,0:T(8,128)}), f32[64,7168]{1,0:T(8,128)}) %all-reduce.6.cloned.1.call-update) | async-done | bytes 1835024 | tf_op jit(solution)/shard_map/psum | solution.py:164
  440.9 1.7 multiply_reduce_fusion
  442.6 2.7 multiply_convert_fusion
  446.2 1.6 dynamic-slice_convert_fusion
  447.9 43.0 %all-gather.13.cloned.1.call-done = bf16[512,7168]{1,0:T(8,128)(2,1)} async-done(((bf16[64,7168]{1,0:T(8,128)(2,1)}), bf16[512,7168]{1,0:T(8,128)(2,1)}) %all-gather.13.cloned.1.call-update) | async-done | bytes 7340048 | tf_op jit(solution)/shard_map/all_gather | solution.py:176
  490.8 8.5 %fusion.98 = (f32[512]{0:T(512)S(1)}, f32[512,512]{0,1:T(8,128)S(1)}) fusion(bf16[512,7168]{1,0:T(8,128)(2,1)} %all-gather.13.cloned.1.call-done, bf16[512,7168]{1,0:T(8,128)(2,1)} %param.27), kind=kOutput, calls=%fused_computation.170 | convolution fusion | flops 3758358016 | bytes 15730688 | tf_op jit(solution)/shard_map/rd,vd->rv/dot_general | solution.py:174
  499.4 0.3 copy.58
  499.7 0.2 exponential_reduce_fusion
  499.9 1.6 gather_fusion
  501.5 0.3 select_reduce_fusion
  501.8 9.6 %all-gather.4 = f32[4,3,512]{2,1,0:T(4,128)S(1)} all-gather(f32[1,3,512]{2,1,0:T(4,128)S(1)} %maximum_bitcast_fusion.1), channel_id=2, replica_groups=mesh['seq_0'=4,'seq_1'=4,'batch_0'=4,'batch_1'=2] {'seq_0'}, dimensions={0}, use_global_device_ids=true | all-gather | bytes 30720 | tf_op jit(solution)/shard_map/all_gather | solution.py:43
  511.4 9.5 %all-gather.5 = f32[4,3,512]{2,1,0:T(4,128)S(1)} all-gather(f32[1,3,512]{2,1,0:T(4,128)S(1)} %maximum_bitcast_fusion.2), channel_id=3, replica_groups=mesh['seq_0'=4,'seq_1'=4,'batch_0'=4,'batch_1'=2] {'seq_1'}, dimensions={0}, use_global_device_ids=true | all-gather | bytes 30720 | tf_op jit(solution)/shard_map/all_gather | solution.py:43
  521.0 9.0 %all-gather.6 = f32[4,3,512]{2,1,0:T(4,128)S(1)} all-gather(f32[1,3,512]{2,1,0:T(4,128)S(1)} %maximum_bitcast_fusion.3), channel_id=4, replica_groups=mesh['seq_0'=4,'seq_1'=4,'batch_0'=4,'batch_1'=2] {'batch_0'}, dimensions={0}, use_global_device_ids=true | all-gather | bytes 30720 | tf_op jit(solution)/shard_map/all_gather | solution.py:43
  530.1 10.2 %all-gather.7 = f32[2,3,512]{2,1,0:T(4,128)S(1)} all-gather(f32[1,3,512]{2,1,0:T(4,128)S(1)} %maximum_bitcast_fusion.4), channel_id=5, replica_groups=mesh['seq_0'=4,'seq_1'=4,'batch_0'=4,'batch_1'=2] {'batch_1'}, dimensions={0}, use_global_device_ids=true | all-gather | bytes 18432 | tf_op jit(solution)/shard_map/all_gather | solution.py:43
  540.3 3.5 gather_fusion.1
  544.0 1.1 fusion.89
  (80 shorter events, 2.8 us)
Async XLA Ops:
  7.2 113.3 %copy-start = (bf16[1,1024,512]{2,1,0:T(8,128)(2,1)S(1)}, bf16[1,1024,512]{2,1,0:T(8,128)(2,1)}, u32[]{:S(2)}) copy-start(bf16[1,1024,512]{2,1,0:T(8,128)(2,1)} %param.20) | copy-start | bytes 3145732
  7.2 92.3 %copy-start.5 = (bf16[1,64,512]{2,1,0:T(8,128)(2,1)S(1)}, bf16[1,64,512]{2,1,0:T(8,128)(2,1)}, u32[]{:S(2)}) copy-start(bf16[1,64,512]{2,1,0:T(8,128)(2,1)} %param.22) | copy-start | bytes 196612
  7.2 87.5 %all-gather.11.cloned.1.call-start = ((), (), s32[]{:S(2)}) async-start(), calls=%async_computation.2 | async-start | bytes 11141120 | tf_op jit(solution)/shard_map/all_gather | solution.py:22
  10.8 306.5 %reduce-scatter.3.cloned.1.call-start = ((), (), s32[]{:S(2)}) async-start(), calls=%async_computation.3 | async-start | bytes 17825792 | tf_op jit(solution)/shard_map/reduce_scatter | solution.py:146
  96.5 10.4 %copy-start.8 = (bf16[1,64,64]{2,1,0:T(8,128)(2,1)S(1)}, bf16[1,64,64]{2,1,0:T(8,128)(2,1)}, u32[]{:S(2)}) copy-start(bf16[1,64,64]{2,1,0:T(8,128)(2,1)} %param.23) | copy-start | bytes 24580
  120.5 30.0 %copy-start.3 = (bf16[1,64,128,64]{2,3,1,0:T(8,128)(2,1)S(1)}, bf16[1,64,128,64]{2,3,1,0:T(8,128)(2,1)}, u32[]{:S(2)}) copy-start(bf16[1,64,128,64]{2,3,1,0:T(8,128)(2,1)} %copy.69) | copy-start | bytes 3145732
  120.5 30.0 %copy-start.4 = (bf16[1,1024,64]{1,2,0:T(8,128)(2,1)S(1)}, bf16[1,1024,64]{1,2,0:T(8,128)(2,1)}, u32[]{:S(2)}) copy-start(bf16[1,1024,64]{1,2,0:T(8,128)(2,1)} %param.21) | copy-start | bytes 393220
  206.4 0.7 copy-start.12
  206.4 177.7 %all-reduce.4.cloned.1.call-start = ((), (), s32[]{:S(2)}) async-start(), calls=%async_computation.4 | async-start | bytes 3670016 | tf_op jit(solution)/shard_map/psum | solution.py:164
  209.5 109.3 %copy-start.11 = (bf16[8,512,128]{2,1,0:T(8,128)(2,1)S(1)}, bf16[8,512,128]{2,1,0:T(8,128)(2,1)}, u32[]{:S(2)}) copy-start(bf16[8,512,128]{2,1,0:T(8,128)(2,1)} %param.19) | copy-start | bytes 3145732
  319.3 7.9 %copy-start.6 = (bf16[64,448]{1,0:T(8,128)(2,1)S(1)}, bf16[64,448]{1,0:T(8,128)(2,1)}, u32[]{:S(2)}) copy-start(bf16[64,448]{1,0:T(8,128)(2,1)} %param.24) | copy-start | bytes 172036
  319.3 123.3 %copy-start.7 = (f32[7168]{0:T(1024)S(1)}, f32[7168]{0:T(1024)}, u32[]{:S(2)}) copy-start(f32[7168]{0:T(1024)} %param.26) | copy-start | bytes 86020
  327.2 118.7 %copy-start.9 = (s32[8,64]{1,0:T(8,128)S(1)}, s32[8,64]{1,0:T(8,128)}, u32[]{:S(2)}) copy-start(s32[8,64]{1,0:T(8,128)} %param.29) | copy-start | bytes 6148
  327.2 118.8 %copy-start.10 = (s32[8,64]{1,0:T(8,128)S(1)}, s32[8,64]{1,0:T(8,128)}, u32[]{:S(2)}) copy-start(s32[8,64]{1,0:T(8,128)} %param.28) | copy-start | bytes 6148
  328.5 1.2 copy-start.2
  329.7 111.1 %all-reduce.6.cloned.1.call-start = ((), (), s32[]{:S(2)}) async-start(), calls=%async_computation.5 | async-start | bytes 3670016 | tf_op jit(solution)/shard_map/psum | solution.py:164
  384.1 106.7 %all-gather.13.cloned.1.call-start = ((), (), s32[]{:S(2)}) async-start(), calls=%async_computation.6 | async-start | bytes 8257536 | tf_op jit(solution)/shard_map/all_gather | solution.py:176
  490.8 54.3 %copy-start.1 = (bf16[1,1024,512]{2,1,0:T(8,128)(2,1)S(1)}, bf16[1,1024,512]{2,1,0:T(8,128)(2,1)}, u32[]{:S(2)}) copy-start(bf16[1,1024,512]{2,1,0:T(8,128)(2,1)} %param.20) | copy-start | bytes 3145732
Sparse Core Ops, SparseCore 0:
  10.9 83.7 all-gather.10
  206.5 110.7 reduce-scatter.2
  329.8 54.2 all-reduce.3
  386.3 54.4 all-reduce.5
  445.4 45.3 all-gather.12
